TPU v7x, 32 devices: a whole 2x2x4 slice. The times are simulated.
32 devices in a mesh: src: 8 (over z, x), tgt: 4 (over y, core).
Axes of the slice: x: 2, y: 2, z: 4, core: 2. Of those that a mesh axis runs over, the one named last changes fastest.
Arguments:
- source_words: bfloat16 [4096, 300], P(('src', 'tgt')), may hold values from -3 to 3
- target_words: bfloat16 [3840, 300], P(('tgt', 'src')), may hold values from -24 to 24
Outputs:
- rotated: bfloat16 [4096, 300], P(('src', 'tgt'))
- matched: float32 [4096, 300], P(('src', 'tgt'))
- ortho: float32 [300, 300], replicated
- row_pot: float32 [4096], P(('src', 'tgt'))
- col_pot: float32 [3840], P(('tgt', 'src'))
All inputs are finite; a program needn't handle non-finite values.
Results may differ from a plain program's by a relative error of at most 0.0034.
Values may be sent and summed in bfloat16 or wider, within the bound.
No kernel may reach another device: no remote copies, remote signals or barrier semaphores. Data moves between devices by JAX's collectives and lax.ppermute only.
A program may use at most 64 MiB of HBM per device.

v0:
```python
import math
import jax
import jax.numpy as jnp
from jax import lax
from jax.sharding import PartitionSpec as P

ITERS = 2
NEWTON = 12


def reduce_rows(top, total):
    higher = lax.pmax(top, "tgt")
    whole = lax.psum(total * jnp.exp(top - higher), "tgt")
    return -(higher + jnp.log(whole))


def reduce_cols(top, total):
    higher = lax.pmax(top, "src")
    whole = lax.psum(total * jnp.exp(top - higher), "src")
    return -(higher + jnp.log(whole))


def body(source_words, target_words):
    width = source_words.shape[1]
    scale = 4.0 / math.sqrt(width)
    highest = lax.Precision.HIGHEST
    src_block = lax.all_gather(source_words, "tgt", axis=0, tiled=True)
    rows = src_block.shape[0]
    cols = target_words.shape[0] * lax.axis_size("src")
    inner = (((1,), (1,)), ((), ()))
    leading = (((0,), (0,)), ((), ()))

    def scores(piece):
        return lax.dot_general(src_block, piece, inner, preferred_element_type=jnp.float32) * scale

    col_pot = jnp.zeros((cols,), jnp.float32)
    row_pot = jnp.zeros((rows,), jnp.float32)
    for sweep_index in range(ITERS):
        row_top = jnp.full((rows,), -jnp.inf, jnp.float32)
        total = jnp.zeros((rows,), jnp.float32)
        row_shift = col_pot
        row_logits = (
            scores(lax.all_gather(target_words, "src", axis=0, tiled=True)) + row_shift[None, :]
        )
        higher = jnp.max(row_logits, axis=1)
        total = total * jnp.exp(row_top - higher) + jnp.sum(
            jnp.exp(row_logits - higher[:, None]), axis=1
        )
        top, total = (higher, total)
        row_pot = reduce_rows(top, total)
        logits = scores(lax.all_gather(target_words, "src", axis=0, tiled=True)) + row_pot[:, None]
        col_top = jnp.max(logits, axis=0)
        parts = jnp.stack([col_top, jnp.sum(jnp.exp(logits - col_top[None, :]), axis=0)])
        col_pot = reduce_cols(parts[0], parts[1])
    piece = lax.all_gather(target_words, "src", axis=0, tiled=True)
    plan = jnp.exp(scores(piece) + row_pot[:, None] + col_pot[None, :]).astype(jnp.bfloat16)
    summed = jnp.dot(plan, piece, preferred_element_type=jnp.float32)
    matched = lax.psum_scatter(summed, "tgt", scatter_dimension=0, tiled=True)
    term = lax.dot_general(source_words.astype(jnp.float32), matched, leading, precision=highest)
    cov = lax.psum(term, ("src", "tgt"))
    ortho = cov / jnp.sqrt(jnp.sum(cov * cov) + 1e-06)
    for step_index in range(NEWTON):
        ortho = 1.5 * ortho - 0.5 * jnp.dot(
            ortho, jnp.dot(ortho.T, ortho, precision=highest), precision=highest
        )
    rotated = jnp.dot(source_words.astype(jnp.float32), ortho, precision=highest).astype(
        jnp.bfloat16
    )
    own_rows = rows // lax.axis_size("tgt")
    own_cols = cols // lax.axis_size("src")
    row_part = lax.dynamic_slice_in_dim(row_pot, lax.axis_index("tgt") * own_rows, own_rows)
    col_part = lax.dynamic_slice_in_dim(col_pot, lax.axis_index("src") * own_cols, own_cols)
    return (rotated, matched, ortho, row_part, col_part)


def solution(mesh):
    in_specs = (P(("src", "tgt"), None), P(("tgt", "src"), None))
    out_specs = (
        P(("src", "tgt"), None),
        P(("src", "tgt"), None),
        P(),
        P(("src", "tgt")),
        P(("tgt", "src")),
    )
    return jax.shard_map(body, mesh=mesh, in_specs=in_specs, out_specs=out_specs, check_vma=False)
```

profile of v0, /device:TPU:0, one launch (start us, length us, event | category | flops | bytes accessed | tf_op | source)
XLA Modules:
  0.0 346.5 jit_solution(8478248790256403142)
XLA Ops:
  7.2 33.5 %all-gather = bf16[8,120,300]{1,2,0:T(8,128)(2,1)S(1)} all-gather(bf16[1,120,300]{1,2,0:T(8,128)(2,1)} %bitcast.59), channel_id=1, replica_groups=mesh['src'=8,'tgt'=4] {'src'}, dimensions={0}, use_global_device_ids=true | all-gather | bytes 648000 | tf_op jit(solution)/shard_map/all_gather | solution.py:55
  40.9 0.5 reshape.19
  41.4 6.1 %all_gather.4 = bf16[512,300]{0,1:T(8,128)(2,1)S(1)} all-gather(bf16[128,300]{0,1:T(8,128)(2,1)S(1)} %copy-done), channel_id=1, replica_groups=mesh['src'=8,'tgt'=4] {'tgt'}, dimensions={0}, use_global_device_ids=true | all-gather | bytes 384000 | tf_op jit(solution)/shard_map/all_gather | solution.py:27
  47.5 0.7 fusion.17
  48.3 7.0 %pmax.28 = f32[512]{0:T(512)S(1)} all-reduce(f32[512]{0:T(512)S(1)} %get-tuple-element.20), channel_id=1, replica_groups=mesh['src'=8,'tgt'=4] {'tgt'}, use_global_device_ids=true, to_apply=%region_1.0 | all-reduce | flops 512 | bytes 4096 | tf_op jit(solution)/shard_map/pmax | solution.py:12
  55.6 5.7 %psum.35 = f32[512]{0:T(512)S(1)} all-reduce(f32[512]{0:T(512)S(1)} %exponential_multiply_fusion.3), channel_id=1, replica_groups=mesh['src'=8,'tgt'=4] {'tgt'}, use_global_device_ids=true, to_apply=%region_3.0 | all-reduce | flops 512 | bytes 4096 | tf_op jit(solution)/shard_map/psum | solution.py:13
  61.5 0.6 exponential_reduce_fusion.2
  62.0 21.5 %pmax.29 = f32[960]{0:T(1024)S(1)} all-reduce(f32[960]{0:T(1024)S(1)} %add_reduce_fusion.1), channel_id=1, replica_groups=mesh['src'=8,'tgt'=4] {'src'}, use_global_device_ids=true, to_apply=%region_5.0 | all-reduce | flops 960 | bytes 7680 | tf_op jit(solution)/shard_map/pmax | solution.py:18
  83.5 17.1 %psum.36 = f32[960]{0:T(1024)S(1)} all-reduce(f32[960]{0:T(1024)S(1)} %exponential_multiply_fusion.1), channel_id=1, replica_groups=mesh['src'=8,'tgt'=4] {'src'}, use_global_device_ids=true, to_apply=%region_7.0 | all-reduce | flops 960 | bytes 7680 | tf_op jit(solution)/shard_map/psum | solution.py:19
  100.9 0.4 exponential_reduce_fusion.1
  101.3 5.7 %pmax.30 = f32[512]{0:T(512)S(1)} all-reduce(f32[512]{0:T(512)S(1)} %add_reduce_fusion), channel_id=1, replica_groups=mesh['src'=8,'tgt'=4] {'tgt'}, use_global_device_ids=true, to_apply=%region_9.0 | all-reduce | flops 512 | bytes 4096 | tf_op jit(solution)/shard_map/pmax | solution.py:12
  107.0 6.0 %psum.37 = f32[512]{0:T(512)S(1)} all-reduce(f32[512]{0:T(512)S(1)} %exponential_multiply_fusion.2), channel_id=1, replica_groups=mesh['src'=8,'tgt'=4] {'tgt'}, use_global_device_ids=true, to_apply=%region_11.0 | all-reduce | flops 512 | bytes 4096 | tf_op jit(solution)/shard_map/psum | solution.py:13
  113.3 0.6 exponential_reduce_fusion
  113.8 19.1 %pmax.31 = f32[960]{0:T(1024)S(1)} all-reduce(f32[960]{0:T(1024)S(1)} %add_reduce_fusion.2), channel_id=1, replica_groups=mesh['src'=8,'tgt'=4] {'src'}, use_global_device_ids=true, to_apply=%region_13.0 | all-reduce | flops 960 | bytes 7680 | tf_op jit(solution)/shard_map/pmax | solution.py:18
  133.0 17.2 %psum.38 = f32[960]{0:T(1024)S(1)} all-reduce(f32[960]{0:T(1024)S(1)} %exponential_multiply_fusion), channel_id=1, replica_groups=mesh['src'=8,'tgt'=4] {'src'}, use_global_device_ids=true, to_apply=%region_15.0 | all-reduce | flops 960 | bytes 7680 | tf_op jit(solution)/shard_map/psum | solution.py:19
  150.2 1.4 fusion.13
  151.9 20.7 %reduce-scatter.2.cloned.1.call-done = f32[128,300]{0,1:T(8,128)} async-done(((f32[512,300]{0,1:T(8,128)}), f32[128,300]{0,1:T(8,128)}) %reduce-scatter.2.cloned.1.call-update) | async-done | bytes 153616 | tf_op jit(solution)/shard_map/reduce_scatter | solution.py:58
  172.5 2.0 convolution_bitcast_fusion
  174.6 0.6 dynamic_slice.7
  175.2 0.6 dynamic_slice.6
  175.7 130.6 %all-reduce.2.cloned.1.call-done = f32[300,300]{0,1:T(8,128)} async-done(((f32[300,300]{0,1:T(8,128)}), f32[300,300]{0,1:T(8,128)}) %all-reduce.2.cloned.1.call-update) | async-done | bytes 360016 | tf_op jit(solution)/shard_map/psum | solution.py:60
  306.3 1.8 multiply_reduce_fusion
  308.8 2.2 fusion.16
  311.1 1.2 fusion.11
  312.3 1.0 fusion.18
  313.4 1.2 fusion.10
  314.6 1.0 fusion.19
  315.6 1.2 fusion.9
  316.8 1.0 fusion.20
  317.9 1.2 fusion.8
  319.1 1.0 fusion.21
  320.1 1.2 fusion.7
  321.4 1.3 fusion.22
  322.6 1.2 fusion.6
  323.8 1.0 fusion.23
  324.9 1.2 fusion.5
  326.1 1.0 fusion.24
  327.2 1.2 fusion.4
  328.4 1.0 fusion.25
  329.4 1.2 fusion.3
  330.6 1.0 fusion.26
  331.7 1.2 fusion.2
  332.9 1.3 fusion.27
  334.2 1.2 fusion.1
  335.4 1.0 fusion.28
  336.4 1.2 fusion
  337.7 1.0 copy.47
  338.7 1.0 fusion.12
  (21 shorter events, 1.5 us)
Async XLA Ops:
  7.2 34.2 %copy-start = (bf16[128,300]{0,1:T(8,128)(2,1)S(1)}, bf16[128,300]{0,1:T(8,128)(2,1)}, u32[]{:S(2)}) copy-start(bf16[128,300]{0,1:T(8,128)(2,1)} %param.2) | copy-start | bytes 230404
  7.2 165.4 %reduce-scatter.2.cloned.1.call-start = ((), (), s32[]{:S(2)}) async-start(), calls=%async_computation.1 | async-start | bytes 778240 | tf_op jit(solution)/shard_map/reduce_scatter | solution.py:58
  151.6 154.7 %all-reduce.2.cloned.1.call-start = ((), (), s32[]{:S(2)}) async-start(), calls=%async_computation.2 | async-start | bytes 933888 | tf_op jit(solution)/shard_map/psum | solution.py:60
  306.3 4.8 %copy-start.1 = (f32[300,300]{0,1:T(8,128)S(1)}, f32[300,300]{0,1:T(8,128)}, u32[]{:S(2)}) copy-start(f32[300,300]{0,1:T(8,128)} %all-reduce.2.cloned.1.call-done) | copy-start | bytes 1080004
Sparse Core Ops, SparseCore 0:
  151.7 20.7 reduce-scatter.1
  178.4 127.8 all-reduce.1
where the time goes:
time: 347 us; the launch traced here: 346 us
  waiting for transfers between devices  151 us (44%)
  blocking collectives  139 us (40%)
  matrix products  33.8 us (10%)
  between operations  15 us (4%)
  other arithmetic  4.41 us (1%)
    psum x1, waiting for transfers between devices, body(): cov = lax.psum(term, ('src', 'tgt'))  131 us
    pmax x2, blocking collectives, reduce_cols(): higher = lax.pmax(top, 'src')  40.6 us
    psum x2, blocking collectives, reduce_cols(): whole = lax.psum(total * jnp.exp(top - higher), 'src')  34.3 us
    all_gather x1, blocking collectives, body(): piece = lax.all_gather(target_words, 'src', axis=0, tiled=True)  33.5 us
    reduce_scatter x1, waiting for transfers between devices, body(): matched = lax.psum_scatter(summed, 'tgt', scatter_dimension=0, tiled=True)  20.7 us
    dot_general x12, matrix products, body(): jnp.dot(ortho, jnp.dot(ortho.T, ortho, precision=highest), precision=high...  14.5 us
    dot_general x12, matrix products, body(): jnp.dot(ortho.T, ortho, precision=highest)  14.1 us
    pmax x2, blocking collectives, reduce_rows(): higher = lax.pmax(top, 'tgt')  12.6 us
  transfers between devices with their start and end apart: 2, of which 2 were waited for; matrix products, arithmetic and copies ran while one was open for 0% of the time, Pallas kernels for 0%

commit v1 on v0

--- a/solution.py
+++ b/solution.py
@@ -57,7 +57,7 @@
     summed = jnp.dot(plan, piece, preferred_element_type=jnp.float32)
     matched = lax.psum_scatter(summed, "tgt", scatter_dimension=0, tiled=True)
     term = lax.dot_general(source_words.astype(jnp.float32), matched, leading, precision=highest)
-    cov = lax.psum(term, ("src", "tgt"))
+    cov = lax.psum(lax.psum(term, "tgt"), "src")
     ortho = cov / jnp.sqrt(jnp.sum(cov * cov) + 1e-06)
     for step_index in range(NEWTON):
         ortho = 1.5 * ortho - 0.5 * jnp.dot(

time: 347 us -> 325 us (0.937)
  waiting for transfers between devices: 151 us -> 129 us
    psum x1 -> x2, waiting for transfers between devices: 131 us -> 109 us  [body(): cov = lax.psum(lax.psum(term, 'tgt'), 'src')]
  transfers between devices with their start and end apart: 2 -> 3, of which waited for: 2 -> 3; matrix products, arithmetic and copies ran while one was open for 0% -> 0% of each run, Pallas kernels for 0% -> 0%
where the time goes in v1:
time: 325 us; the launch traced here: 324 us
  blocking collectives  139 us (43%)
  waiting for transfers between devices  129 us (40%)
  matrix products  33.8 us (10%)
  between operations  14.7 us (5%)
  other arithmetic  4.41 us (1%)
    psum x2, waiting for transfers between devices, body(): cov = lax.psum(lax.psum(term, 'tgt'), 'src')  109 us
    pmax x2, blocking collectives, reduce_cols(): higher = lax.pmax(top, 'src')  40.6 us
    psum x2, blocking collectives, reduce_cols(): whole = lax.psum(total * jnp.exp(top - higher), 'src')  34.3 us
    all_gather x1, blocking collectives, body(): piece = lax.all_gather(target_words, 'src', axis=0, tiled=True)  33.5 us
    reduce_scatter x1, waiting for transfers between devices, body(): matched = lax.psum_scatter(summed, 'tgt', scatter_dimension=0, tiled=True)  20.9 us
    dot_general x12, matrix products, body(): jnp.dot(ortho, jnp.dot(ortho.T, ortho, precision=highest), precision=high...  14.8 us
    dot_general x12, matrix products, body(): jnp.dot(ortho.T, ortho, precision=highest)  13.9 us
    pmax x2, blocking collectives, reduce_rows(): higher = lax.pmax(top, 'tgt')  12.6 us
  transfers between devices with their start and end apart: 3, of which 3 were waited for; matrix products, arithmetic and copies ran while one was open for 0% of the time, Pallas kernels for 0%

profile of v1, /device:TPU:0, one launch (start us, length us, event | category | flops | bytes accessed | tf_op | source)
XLA Modules:
  0.0 324.4 jit_solution(1788646350662916822)
XLA Ops:
  7.2 33.5 %all-gather = bf16[8,120,300]{1,2,0:T(8,128)(2,1)S(1)} all-gather(bf16[1,120,300]{1,2,0:T(8,128)(2,1)} %bitcast.59), channel_id=1, replica_groups=mesh['src'=8,'tgt'=4] {'src'}, dimensions={0}, use_global_device_ids=true | all-gather | bytes 648000 | tf_op jit(solution)/shard_map/all_gather | solution.py:55
  40.9 0.5 reshape.19
  41.4 6.1 %all_gather.4 = bf16[512,300]{0,1:T(8,128)(2,1)S(1)} all-gather(bf16[128,300]{0,1:T(8,128)(2,1)S(1)} %copy-done), channel_id=1, replica_groups=mesh['src'=8,'tgt'=4] {'tgt'}, dimensions={0}, use_global_device_ids=true | all-gather | bytes 384000 | tf_op jit(solution)/shard_map/all_gather | solution.py:27
  47.5 0.7 fusion.17
  48.3 7.0 %pmax.28 = f32[512]{0:T(512)S(1)} all-reduce(f32[512]{0:T(512)S(1)} %get-tuple-element.20), channel_id=1, replica_groups=mesh['src'=8,'tgt'=4] {'tgt'}, use_global_device_ids=true, to_apply=%region_1.0 | all-reduce | flops 512 | bytes 4096 | tf_op jit(solution)/shard_map/pmax | solution.py:12
  55.6 5.7 %psum.42 = f32[512]{0:T(512)S(1)} all-reduce(f32[512]{0:T(512)S(1)} %exponential_multiply_fusion.3), channel_id=1, replica_groups=mesh['src'=8,'tgt'=4] {'tgt'}, use_global_device_ids=true, to_apply=%region_3.0 | all-reduce | flops 512 | bytes 4096 | tf_op jit(solution)/shard_map/psum | solution.py:13
  61.5 0.6 exponential_reduce_fusion.2
  62.0 21.5 %pmax.29 = f32[960]{0:T(1024)S(1)} all-reduce(f32[960]{0:T(1024)S(1)} %add_reduce_fusion.1), channel_id=1, replica_groups=mesh['src'=8,'tgt'=4] {'src'}, use_global_device_ids=true, to_apply=%region_5.0 | all-reduce | flops 960 | bytes 7680 | tf_op jit(solution)/shard_map/pmax | solution.py:18
  83.5 17.1 %psum.43 = f32[960]{0:T(1024)S(1)} all-reduce(f32[960]{0:T(1024)S(1)} %exponential_multiply_fusion.1), channel_id=1, replica_groups=mesh['src'=8,'tgt'=4] {'src'}, use_global_device_ids=true, to_apply=%region_7.0 | all-reduce | flops 960 | bytes 7680 | tf_op jit(solution)/shard_map/psum | solution.py:19
  101.3 5.7 %pmax.30 = f32[512]{0:T(512)S(1)} all-reduce(f32[512]{0:T(512)S(1)} %add_reduce_fusion), channel_id=1, replica_groups=mesh['src'=8,'tgt'=4] {'tgt'}, use_global_device_ids=true, to_apply=%region_9.0 | all-reduce | flops 512 | bytes 4096 | tf_op jit(solution)/shard_map/pmax | solution.py:12
  107.0 6.0 %psum.44 = f32[512]{0:T(512)S(1)} all-reduce(f32[512]{0:T(512)S(1)} %exponential_multiply_fusion.2), channel_id=1, replica_groups=mesh['src'=8,'tgt'=4] {'tgt'}, use_global_device_ids=true, to_apply=%region_11.0 | all-reduce | flops 512 | bytes 4096 | tf_op jit(solution)/shard_map/psum | solution.py:13
  113.3 0.6 exponential_reduce_fusion
  113.8 19.1 %pmax.31 = f32[960]{0:T(1024)S(1)} all-reduce(f32[960]{0:T(1024)S(1)} %add_reduce_fusion.2), channel_id=1, replica_groups=mesh['src'=8,'tgt'=4] {'src'}, use_global_device_ids=true, to_apply=%region_13.0 | all-reduce | flops 960 | bytes 7680 | tf_op jit(solution)/shard_map/pmax | solution.py:18
  133.0 17.2 %psum.45 = f32[960]{0:T(1024)S(1)} all-reduce(f32[960]{0:T(1024)S(1)} %exponential_multiply_fusion), channel_id=1, replica_groups=mesh['src'=8,'tgt'=4] {'src'}, use_global_device_ids=true, to_apply=%region_15.0 | all-reduce | flops 960 | bytes 7680 | tf_op jit(solution)/shard_map/psum | solution.py:19
  150.2 1.4 fusion.13
  151.7 20.9 %reduce-scatter.2.cloned.1.call-done = f32[128,300]{0,1:T(8,128)} async-done(((f32[512,300]{0,1:T(8,128)}), f32[128,300]{0,1:T(8,128)}) %reduce-scatter.2.cloned.1.call-update) | async-done | bytes 153616 | tf_op jit(solution)/shard_map/reduce_scatter | solution.py:58
  172.5 2.0 convolution_bitcast_fusion
  174.8 33.7 %all-reduce.3.cloned.1.call-done = f32[300,300]{0,1:T(8,128)} async-done(((f32[300,300]{0,1:T(8,128)}), f32[300,300]{0,1:T(8,128)}) %all-reduce.3.cloned.1.call-update) | async-done | bytes 360016 | tf_op jit(solution)/shard_map/psum | solution.py:60
  208.5 0.6 dynamic_slice.7
  209.1 0.6 dynamic_slice.6
  209.6 74.9 %all-reduce.5.cloned.1.call-done = f32[300,300]{0,1:T(8,128)} async-done(((f32[300,300]{0,1:T(8,128)}), f32[300,300]{0,1:T(8,128)}) %all-reduce.5.cloned.1.call-update) | async-done | bytes 360016 | tf_op jit(solution)/shard_map/psum | solution.py:60
  284.5 1.8 multiply_reduce_fusion
  287.0 2.2 fusion.16
  289.3 1.2 fusion.11
  290.5 1.0 fusion.18
  291.6 1.2 fusion.10
  292.8 1.0 fusion.19
  293.8 1.2 fusion.9
  295.0 1.0 fusion.20
  296.1 1.2 fusion.8
  297.3 1.0 fusion.21
  298.3 1.2 fusion.7
  299.6 1.3 fusion.22
  300.8 1.2 fusion.6
  302.0 1.0 fusion.23
  303.1 1.2 fusion.5
  304.3 1.0 fusion.24
  305.4 1.2 fusion.4
  306.6 1.0 fusion.25
  307.6 1.2 fusion.3
  308.8 1.0 fusion.26
  309.9 1.2 fusion.2
  311.1 1.0 fusion.27
  312.1 1.5 fusion.1
  313.6 1.0 fusion.28
  314.6 1.2 fusion
  315.9 1.0 copy.47
  316.9 1.0 fusion.12
  (24 shorter events, 2.0 us)
Async XLA Ops:
  7.2 34.2 %copy-start = (bf16[128,300]{0,1:T(8,128)(2,1)S(1)}, bf16[128,300]{0,1:T(8,128)(2,1)}, u32[]{:S(2)}) copy-start(bf16[128,300]{0,1:T(8,128)(2,1)} %param.2) | copy-start | bytes 230404
  7.2 165.4 %reduce-scatter.2.cloned.1.call-start = ((), (), s32[]{:S(2)}) async-start(), calls=%async_computation.1 | async-start | bytes 778240 | tf_op jit(solution)/shard_map/reduce_scatter | solution.py:58
  151.6 56.8 %all-reduce.3.cloned.1.call-start = ((), (), s32[]{:S(2)}) async-start(), calls=%async_computation.2 | async-start | bytes 933888 | tf_op jit(solution)/shard_map/psum | solution.py:60
  174.6 110.0 %all-reduce.5.cloned.1.call-start = ((), (), s32[]{:S(2)}) async-start(), calls=%async_computation.3 | async-start | bytes 933888 | tf_op jit(solution)/shard_map/psum | solution.py:60
  284.5 4.8 %copy-start.1 = (f32[300,300]{0,1:T(8,128)S(1)}, f32[300,300]{0,1:T(8,128)}, u32[]{:S(2)}) copy-start(f32[300,300]{0,1:T(8,128)} %all-reduce.5.cloned.1.call-done) | copy-start | bytes 1080004
Sparse Core Ops, SparseCore 0:
  151.7 20.7 reduce-scatter.1
  175.5 32.9 all-reduce.2
  211.9 72.6 all-reduce.4

commit v2 on v0

--- a/solution.py
+++ b/solution.py
@@ -16,7 +16,7 @@
 
 def reduce_cols(top, total):
     higher = lax.pmax(top, "src")
-    whole = lax.psum(total * jnp.exp(top - higher), "src")
+    whole = jnp.sum(lax.all_gather(total * jnp.exp(top - higher), "src"), axis=0)
     return -(higher + jnp.log(whole))
 
 

time: 347 us -> 379 us (1.092)
  blocking collectives: 139 us -> 170 us
    unnamed x0 -> x2, blocking collectives: none -> 67.9 us
    psum x2 -> x0, blocking collectives: 34.3 us -> none  [reduce_cols(): whole = lax.psum(total * jnp.exp(top - higher), 'src')]
where the time goes in v2:
time: 379 us; the launch traced here: 378 us
  blocking collectives  170 us (45%)
  waiting for transfers between devices  150 us (40%)
  matrix products  33.8 us (9%)
  between operations  15.7 us (4%)
  other arithmetic  4.67 us (1%)
    psum x1, waiting for transfers between devices, body(): cov = lax.psum(term, ('src', 'tgt'))  131 us
    unnamed x2, blocking collectives  67.9 us
    pmax x2, blocking collectives, reduce_cols(): higher = lax.pmax(top, 'src')  38.6 us
    all_gather x1, blocking collectives, body(): piece = lax.all_gather(target_words, 'src', axis=0, tiled=True)  33.5 us
    reduce_scatter x1, waiting for transfers between devices, body(): matched = lax.psum_scatter(summed, 'tgt', scatter_dimension=0, tiled=True)  19.3 us
    dot_general x12, matrix products, body(): jnp.dot(ortho, jnp.dot(ortho.T, ortho, precision=highest), precision=high...  14.5 us
    dot_general x12, matrix products, body(): jnp.dot(ortho.T, ortho, precision=highest)  14.1 us
    pmax x2, blocking collectives, reduce_rows(): higher = lax.pmax(top, 'tgt')  12.6 us
  transfers between devices with their start and end apart: 2, of which 2 were waited for; matrix products, arithmetic and copies ran while one was open for 0% of the time, Pallas kernels for 0%

profile of v2, /device:TPU:0, one launch (start us, length us, event | category | flops | bytes accessed | tf_op | source)
XLA Modules:
  0.0 378.4 jit_solution(6813428758265139506)
XLA Ops:
  7.2 33.5 %all-gather.2 = bf16[8,120,300]{1,2,0:T(8,128)(2,1)S(1)} all-gather(bf16[1,120,300]{1,2,0:T(8,128)(2,1)} %bitcast.60), channel_id=1, replica_groups=mesh['src'=8,'tgt'=4] {'src'}, dimensions={0}, use_global_device_ids=true | all-gather | bytes 648000 | tf_op jit(solution)/shard_map/all_gather | solution.py:55
  40.9 0.5 reshape.27
  41.4 6.1 %all_gather.22 = bf16[512,300]{0,1:T(8,128)(2,1)S(1)} all-gather(bf16[128,300]{0,1:T(8,128)(2,1)S(1)} %copy-done), channel_id=1, replica_groups=mesh['src'=8,'tgt'=4] {'tgt'}, dimensions={0}, use_global_device_ids=true | all-gather | bytes 384000 | tf_op jit(solution)/shard_map/all_gather | solution.py:27
  47.5 0.7 fusion.17
  48.3 7.0 %pmax.28 = f32[512]{0:T(512)S(1)} all-reduce(f32[512]{0:T(512)S(1)} %get-tuple-element.25), channel_id=1, replica_groups=mesh['src'=8,'tgt'=4] {'tgt'}, use_global_device_ids=true, to_apply=%region_1.0 | all-reduce | flops 512 | bytes 4096 | tf_op jit(solution)/shard_map/pmax | solution.py:12
  55.6 5.7 %psum.21 = f32[512]{0:T(512)S(1)} all-reduce(f32[512]{0:T(512)S(1)} %exponential_multiply_fusion.1), channel_id=1, replica_groups=mesh['src'=8,'tgt'=4] {'tgt'}, use_global_device_ids=true, to_apply=%region_3.0 | all-reduce | flops 512 | bytes 4096 | tf_op jit(solution)/shard_map/psum | solution.py:13
  61.5 0.6 exponential_reduce_fusion.2
  62.0 21.5 %pmax.29 = f32[960]{0:T(1024)S(1)} all-reduce(f32[960]{0:T(1024)S(1)} %add_reduce_fusion.1), channel_id=1, replica_groups=mesh['src'=8,'tgt'=4] {'src'}, use_global_device_ids=true, to_apply=%region_5.0 | all-reduce | flops 960 | bytes 7680 | tf_op jit(solution)/shard_map/pmax | solution.py:18
  83.5 0.6 dynamic-slice
  84.9 33.0 %all-reduce = f32[7680]{0:T(1024)S(1)} all-reduce(f32[7680]{0:T(1024)S(1)} %multiply_dynamic-update-slice_fusion.1), channel_id=2, replica_groups=mesh['src'=8,'tgt'=4] {'src'}, use_global_device_ids=true, to_apply=%add | all-reduce | flops 7680 | bytes 61440
  118.6 5.7 %pmax.30 = f32[512]{0:T(512)S(1)} all-reduce(f32[512]{0:T(512)S(1)} %add_reduce_fusion), channel_id=1, replica_groups=mesh['src'=8,'tgt'=4] {'tgt'}, use_global_device_ids=true, to_apply=%region_9.0 | all-reduce | flops 512 | bytes 4096 | tf_op jit(solution)/shard_map/pmax | solution.py:12
  124.3 6.0 %psum.22 = f32[512]{0:T(512)S(1)} all-reduce(f32[512]{0:T(512)S(1)} %exponential_multiply_fusion), channel_id=1, replica_groups=mesh['src'=8,'tgt'=4] {'tgt'}, use_global_device_ids=true, to_apply=%region_11.0 | all-reduce | flops 512 | bytes 4096 | tf_op jit(solution)/shard_map/psum | solution.py:13
  130.6 0.6 exponential_reduce_fusion
  131.2 17.1 %pmax.31 = f32[960]{0:T(1024)S(1)} all-reduce(f32[960]{0:T(1024)S(1)} %add_reduce_fusion.2), channel_id=1, replica_groups=mesh['src'=8,'tgt'=4] {'src'}, use_global_device_ids=true, to_apply=%region_13.0 | all-reduce | flops 960 | bytes 7680 | tf_op jit(solution)/shard_map/pmax | solution.py:18
  148.4 34.9 %all-reduce.1 = f32[7680]{0:T(1024)S(1)} all-reduce(f32[7680]{0:T(1024)S(1)} %multiply_dynamic-update-slice_fusion), channel_id=3, replica_groups=mesh['src'=8,'tgt'=4] {'src'}, use_global_device_ids=true, to_apply=%add.1 | all-reduce | flops 7680 | bytes 61440
  183.4 1.4 fusion.13
  185.1 19.3 %reduce-scatter.2.cloned.1.call-done = f32[128,300]{0,1:T(8,128)} async-done(((f32[512,300]{0,1:T(8,128)}), f32[128,300]{0,1:T(8,128)}) %reduce-scatter.2.cloned.1.call-update) | async-done | bytes 153616 | tf_op jit(solution)/shard_map/reduce_scatter | solution.py:58
  204.4 2.0 convolution_bitcast_fusion
  206.4 0.6 dynamic_slice.7
  207.0 0.6 dynamic_slice.6
  207.6 130.7 %all-reduce.4.cloned.1.call-done = f32[300,300]{0,1:T(8,128)} async-done(((f32[300,300]{0,1:T(8,128)}), f32[300,300]{0,1:T(8,128)}) %all-reduce.4.cloned.1.call-update) | async-done | bytes 360016 | tf_op jit(solution)/shard_map/psum | solution.py:60
  338.2 1.8 multiply_reduce_fusion
  340.7 2.2 fusion.16
  343.0 1.2 fusion.11
  344.2 1.0 fusion.18
  345.3 1.2 fusion.10
  346.5 1.0 fusion.19
  347.5 1.2 fusion.9
  348.7 1.0 fusion.20
  349.8 1.2 fusion.8
  351.0 1.0 fusion.21
  352.0 1.2 fusion.7
  353.3 1.3 fusion.22
  354.5 1.2 fusion.6
  355.7 1.0 fusion.23
  356.8 1.2 fusion.5
  358.0 1.0 fusion.24
  359.1 1.2 fusion.4
  360.3 1.0 fusion.25
  361.3 1.2 fusion.3
  362.5 1.0 fusion.26
  363.6 1.2 fusion.2
  364.8 1.3 fusion.27
  366.1 1.2 fusion.1
  367.3 1.0 fusion.28
  368.3 1.2 fusion
  369.6 1.0 copy.61
  370.6 1.0 fusion.12
  (30 shorter events, 2.4 us)
Async XLA Ops:
  7.2 34.2 %copy-start = (bf16[128,300]{0,1:T(8,128)(2,1)S(1)}, bf16[128,300]{0,1:T(8,128)(2,1)}, u32[]{:S(2)}) copy-start(bf16[128,300]{0,1:T(8,128)(2,1)} %param.2) | copy-start | bytes 230404
  7.2 197.2 %reduce-scatter.2.cloned.1.call-start = ((), (), s32[]{:S(2)}) async-start(), calls=%async_computation.1 | async-start | bytes 778240 | tf_op jit(solution)/shard_map/reduce_scatter | solution.py:58
  61.3 22.3 %copy-start.2 = (u32[32]{0:T(128)S(1)}, u32[32]{0:T(128)}, u32[]{:S(2)}) copy-start(u32[32]{0:T(128)} %constant.36) | copy-start | bytes 388
  184.9 153.4 %all-reduce.4.cloned.1.call-start = ((), (), s32[]{:S(2)}) async-start(), calls=%async_computation.2 | async-start | bytes 933888 | tf_op jit(solution)/shard_map/psum | solution.py:60
  338.2 4.8 %copy-start.1 = (f32[300,300]{0,1:T(8,128)S(1)}, f32[300,300]{0,1:T(8,128)}, u32[]{:S(2)}) copy-start(f32[300,300]{0,1:T(8,128)} %all-reduce.4.cloned.1.call-done) | copy-start | bytes 1080004
Sparse Core Ops, SparseCore 0:
  185.0 19.3 reduce-scatter.1
  210.2 127.9 all-reduce.3
